TPU v7x, 256 devices: a whole 4x4x8 slice. The times are simulated.
256 devices in a mesh: prow: 16 (over z, core), pcol: 16 (over x, y).
Axes of the slice: x: 4, y: 4, z: 8, core: 2. Of those that a mesh axis runs over, the one named last changes fastest.
Arguments:
- tiles: bfloat16 [32768, 128, 128], P(('prow', 'pcol')), may hold values from -6 to 6
- tile_pos: int32 [32768, 2], P(('prow', 'pcol')), may hold values from -1 to 511, as said below
- pivots: int32 [2, 256], replicated, may hold values from 0 to 255, each once within a row
- inverses: bfloat16 [2, 256, 256], replicated, may hold values from -0.0234375 to 0.0234375
Outputs:
- factored: bfloat16 [32768, 128, 128], P(('prow', 'pcol'))
Inputs may be any that keep to these rules, and one draw needn't show every extreme that they name: `tile_pos`: slot s of device (p, q) (device index p * 16 + q, p along prow) holds a tile (I, J) with I % 16 == p and (J // 2) % 16 == q, or is empty; no tile is listed twice; every tile with I < 4 or J < 4 is listed; listed slots come before empty ones on each device; some device has all 128 slots listed.
All inputs are finite; a program needn't handle non-finite values.
Results may differ from a plain program's by a relative error of at most 0.0067.
Values may be sent and summed in bfloat16 or wider, within the bound.
No kernel may reach another device: no remote copies, remote signals or barrier semaphores. Data moves between devices by JAX's collectives and lax.ppermute only.
A program may use at most 128 MiB of HBM per device.

v0:
```python
import jax
import jax.numpy as jnp
from jax import lax
from jax.sharding import PartitionSpec as P

ROW_TILES = 32


def broadcast(value, axis, root):
    mine = lax.axis_index(axis) == root
    return lax.psum(jnp.where(mine, value, jnp.zeros_like(value)), axis)


def slot_lookup(keys, count):
    targets = jnp.arange(count, dtype=jnp.int32)
    matches = keys[None, :] == targets[:, None]
    positions = jnp.arange(keys.shape[0], dtype=jnp.int32)
    chosen = jnp.sum(jnp.where(matches, positions[None, :], 0), axis=1)
    found = jnp.any(matches, axis=1)
    return (chosen, found)


def local(tiles, tile_pos, pivots, inverses):
    slots, edge, _ = tiles.shape
    row_procs = lax.axis_size("prow")
    col_procs = lax.axis_size("pcol")
    my_col = lax.axis_index("pcol")
    row_tiles = ROW_TILES
    col_tiles = ROW_TILES * row_procs // col_procs
    tile_row = tile_pos[:, 0]
    tile_col = tile_pos[:, 1]
    local_row = jnp.clip(tile_row // row_procs, 0, row_tiles - 1)
    local_col = jnp.clip(2 * (tile_col // 2 // col_procs) + tile_col % 2, 0, col_tiles - 1)
    nothing = jnp.zeros((), jnp.bfloat16)
    current = tiles
    for panel in range(2):
        first = 2 * panel
        in_column = (tile_col >= first) & (tile_col < first + 2)
        col_keys = jnp.where(in_column, local_row * 2 + tile_col - first, -1)
        chosen, found = slot_lookup(col_keys, 2 * row_tiles)
        column = jnp.where(found[:, None, None], current[chosen], nothing)
        column = (
            column.reshape(row_tiles, 2, edge, edge)
            .transpose(0, 2, 1, 3)
            .reshape(row_tiles * edge, 2 * edge)
        )
        inverse = inverses[panel]

        def multiply(block):
            return jnp.dot(block, inverse, preferred_element_type=jnp.float32).astype(jnp.bfloat16)

        def blank(block):
            return jnp.zeros(block.shape, jnp.bfloat16)

        lower = lax.cond(my_col == panel, multiply, blank, column)
        lower = broadcast(lower, "pcol", panel)
        in_block = (tile_row >= first) & (tile_row < first + 2)
        row_keys = jnp.where(in_block, local_col, -1)
        chosen, found = slot_lookup(row_keys, col_tiles)
        mine = jnp.where(found[:, None, None], current[chosen], nothing)
        mine = mine.transpose(1, 0, 2).reshape(edge, col_tiles * edge)
        order = pivots[panel]
        top_rows = broadcast(mine, "prow", first)
        bottom_rows = broadcast(mine, "prow", first + 1)
        upper = jnp.concatenate([top_rows, bottom_rows], axis=0)[order]
        lower_tiles = lower.reshape(row_tiles, edge, 2 * edge)
        upper_tiles = upper.reshape(2 * edge, col_tiles, edge).transpose(1, 0, 2)
        left = lower_tiles[local_row]
        right = upper_tiles[local_col]
        product = jnp.einsum("sik,skj->sij", left, right, preferred_element_type=jnp.float32)
        updated = (current.astype(jnp.float32) - product).astype(jnp.bfloat16)
        lower_parts = lower_tiles.reshape(row_tiles, edge, 2, edge).transpose(0, 2, 1, 3)
        lower_write = lower_parts[local_row, jnp.clip(tile_col - first, 0, 1)]
        upper_parts = upper_tiles.reshape(col_tiles, 2, edge, edge)
        upper_write = upper_parts[local_col, jnp.clip(tile_row - first, 0, 1)]
        trailing = (tile_row >= first + 2) & (tile_col >= first + 2)
        is_lower = in_column & (tile_row >= first + 2)
        current = jnp.where(trailing[:, None, None], updated, current)
        current = jnp.where(is_lower[:, None, None], lower_write, current)
        current = jnp.where(in_block[:, None, None], upper_write, current)
    return current


def solution(mesh):
    return jax.shard_map(
        local,
        mesh=mesh,
        in_specs=(P(("prow", "pcol"), None, None), P(("prow", "pcol"), None), P(), P()),
        out_specs=P(("prow", "pcol"), None, None),
        check_vma=False,
    )
```

profile of v0, /device:TPU:1, one launch (start us, length us, event | category | flops | bytes accessed | tf_op | source)
XLA Modules:
  0.0 537.7 jit_solution(18304019834849628285)
XLA Ops:
  8.3 2.9 gather_fusion
  15.8 4.3 gather_fusion.3
  22.1 2.9 conditional.2
  27.9 106.4 %all-reduce.13.cloned.1.call-done = (bf16[128,4096]{1,0:T(8,128)(2,1)}, bf16[128,4096]{1,0:T(8,128)(2,1)}) async-done(((bf16[128,4096]{1,0:T(8,128)(2,1)}, bf16[128,4096]{1,0:T(8,128)(2,1)}), (bf16[128,4096]{1,0:T(8,128)(2,1)}, bf16[128,4096]{1,0:T(8,128)(2,1)})) %all-reduce.13.cloned.1.call-update) | async-done | bytes 2097168 | tf_op jit(solution)/shard_map/psum | solution.py:11
  136.0 3.2 gather_fusion.1
  139.2 4.0 fusion.42
  143.1 4.7 gather_fusion.2
  147.9 6.8 %gather_fusion.6 = bf16[128,256,128]{2,1,0:T(8,128)(2,1)} fusion(bf16[32,256,128]{2,1,0:T(8,128)(2,1)S(1)} %get-tuple-element.55, s32[1024]{0:T(1024)S(1)} %pad_clamp_fusion.3), kind=kCustom, calls=%fused_computation.6 | custom fusion | bytes 16777728 | tf_op jit(solution)/shard_map/gather | solution.py:69
  154.7 82.7 %all-reduce.7.cloned.1.call-done = bf16[4096,256]{1,0:T(8,128)(2,1)} async-done(((bf16[4096,256]{1,0:T(8,128)(2,1)}), bf16[4096,256]{1,0:T(8,128)(2,1)}) %all-reduce.7.cloned.1.call-update) | async-done | bytes 2097168 | tf_op jit(solution)/shard_map/psum | solution.py:11
  237.3 2.5 reshape.507
  241.7 4.8 gather_fusion.4
  246.5 6.6 %gather_fusion.5 = bf16[128,128,256]{2,1,0:T(8,128)(2,1)} fusion(bf16[32,128,256]{2,1,0:T(8,128)(2,1)S(1)} %bitcast.156, s32[1024]{0:T(1024)S(1)} %pad_clamp_fusion.4), kind=kCustom, calls=%fused_computation.5 | custom fusion | bytes 16777728 | tf_op jit(solution)/shard_map/gather | solution.py:68
  253.1 16.2 %fusion.13 = bf16[128,128,128]{2,1,0:T(8,128)(2,1)} fusion(bf16[128,128,128]{2,1,0:T(8,128)(2,1)} %gather_fusion.2, bf16[128,128,128]{2,1,0:T(8,128)(2,1)} %gather_fusion.4, bf16[128,128,128]{2,1,0:T(8,128)(2,1)} %param.8, pred[128]{0:T(512)(128)(4,1)S(1)} %get-tuple-element.67, pred[128]{0:T(512)(128)(4,1)S(1)} %get-tuple-element.68, ...), kind=kOutput, calls=%fused_computation.31 | convolution fusion | flops 1086324736 | bytes 33554816 | tf_op jit(solution)/shard_map/sik,skj->sij/dot_general | solution.py:70
  269.3 2.9 gather_fusion.7
  276.5 4.4 gather_fusion.10
  284.7 111.6 %all-reduce.11.cloned.1.call-done = (bf16[128,4096]{1,0:T(8,128)(2,1)}, bf16[128,4096]{1,0:T(8,128)(2,1)}) async-done(((bf16[128,4096]{1,0:T(8,128)(2,1)}, bf16[128,4096]{1,0:T(8,128)(2,1)}), (bf16[128,4096]{1,0:T(8,128)(2,1)}, bf16[128,4096]{1,0:T(8,128)(2,1)})) %all-reduce.11.cloned.1.call-update) | async-done | bytes 2097168 | tf_op jit(solution)/shard_map/psum | solution.py:11
  398.0 3.2 gather_fusion.8
  401.2 3.9 fusion.43
  405.1 6.7 %gather_fusion.13 = bf16[128,256,128]{2,1,0:T(8,128)(2,1)} fusion(bf16[32,256,128]{2,1,0:T(8,128)(2,1)S(1)} %get-tuple-element.53, s32[1024]{0:T(1024)S(1)} %pad_clamp_fusion.3), kind=kCustom, calls=%fused_computation.13 | custom fusion | bytes 16777728 | tf_op jit(solution)/shard_map/gather | solution.py:69
  411.8 4.6 gather_fusion.9
  416.4 83.1 %all-reduce.9.cloned.1.call-done = bf16[4096,256]{1,0:T(8,128)(2,1)} async-done(((bf16[4096,256]{1,0:T(8,128)(2,1)}), bf16[4096,256]{1,0:T(8,128)(2,1)}) %all-reduce.9.cloned.1.call-update) | async-done | bytes 2097168 | tf_op jit(solution)/shard_map/psum | solution.py:11
  499.6 8.3 %gather_fusion.12 = bf16[128,128,256]{2,1,0:T(8,128)(2,1)} fusion(bf16[32,128,256]{2,1,0:T(8,128)(2,1)} %bitcast.157, s32[1024]{0:T(1024)S(1)} %pad_clamp_fusion.4), kind=kCustom, calls=%fused_computation.12 | custom fusion | bytes 16777728 | tf_op jit(solution)/shard_map/gather | solution.py:68
  512.1 3.1 gather_fusion.11
  515.2 15.9 %fusion.11 = bf16[128,128,128]{2,1,0:T(8,128)(2,1)} fusion(bf16[128,128,128]{2,1,0:T(8,128)(2,1)} %gather_fusion.9, bf16[128,128,128]{2,1,0:T(8,128)(2,1)} %gather_fusion.11, bf16[128,128,128]{2,1,0:T(8,128)(2,1)} %fusion.13, pred[128]{0:T(512)(128)(4,1)S(1)} %get-tuple-element.66, pred[128]{0:T(512)(128)(4,1)S(1)} %get-tuple-element.64, ...), kind=kOutput, calls=%fused_computation.29 | convolution fusion | flops 1086324736 | bytes 33554816 | tf_op jit(solution)/shard_map/sik,skj->sij/dot_general | solution.py:70
  (69 shorter events, 31.3 us)
Async XLA Ops:
  6.5 127.8 %all-reduce.13.cloned.1.call-start = ((), (), s32[]{:S(2)}) async-start(), calls=%async_computation.3 | async-start | bytes 4194304 | tf_op jit(solution)/shard_map/psum | solution.py:11
  15.5 221.8 %all-reduce.7.cloned.1.call-start = ((), (), s32[]{:S(2)}) async-start(), calls=%async_computation | async-start | bytes 4194304 | tf_op jit(solution)/shard_map/psum | solution.py:11
  20.3 1.9 copy-start.2
  26.5 0.7 copy-start.3
  26.5 0.7 copy-start.4
  26.5 369.8 %all-reduce.11.cloned.1.call-start = ((), (), s32[]{:S(2)}) async-start(), calls=%async_computation.2 | async-start | bytes 4194304 | tf_op jit(solution)/shard_map/psum | solution.py:11
  241.7 4.8 copy-start
  280.8 218.8 %all-reduce.9.cloned.1.call-start = ((), (), s32[]{:S(2)}) async-start(), calls=%async_computation.1 | async-start | bytes 4194304 | tf_op jit(solution)/shard_map/psum | solution.py:11
  499.6 8.3 %copy-start.1 = (bf16[4096,256]{1,0:T(8,128)(2,1)S(1)}, bf16[4096,256]{1,0:T(8,128)(2,1)}, u32[]{:S(2)}) copy-start(bf16[4096,256]{1,0:T(8,128)(2,1)} %all-reduce.9.cloned.1.call-done) | copy-start | bytes 6291460
Sparse Core Ops, SparseCore 0:
  15.6 118.6 all-reduce.12
  137.6 99.6 all-reduce.6
  281.0 115.2 all-reduce.10
  399.8 99.7 all-reduce.8
where the time goes:
time: 538 us
  waiting for transfers between devices  384 us (71%)
  local copies, waits for them, and re-layouts  94.1 us (17%)
  matrix products  32.9 us (6%)
  between operations  13.5 us (3%)
  other arithmetic  12.9 us (2%)
    psum x4, waiting for transfers between devices, broadcast(): return lax.psum(jnp.where(mine, value, jnp.zeros_like(value)), axis)  384 us
    dot_general x2, matrix products, local(): jnp.einsum('sik,skj->sij', left, right, preferred_element_type=jnp.float32)  32.2 us
    gather x2, local copies, waits for them, and re-layouts, local(): left = lower_tiles[local_row]  14.9 us
    gather x2, local copies, waits for them, and re-layouts, local(): right = upper_tiles[local_col]  13.5 us
  transfers between devices with their start and end apart: 4, of which 4 were waited for; matrix products, arithmetic and copies ran while one was open for 10% of the time, Pallas kernels for 0%

commit v1 on v0

--- a/solution.py
+++ b/solution.py
@@ -8,7 +8,7 @@
 
 def broadcast(value, axis, root):
     mine = lax.axis_index(axis) == root
-    return lax.psum(jnp.where(mine, value, jnp.zeros_like(value)), axis)
+    return jnp.sum(lax.all_gather(jnp.where(mine, value, jnp.zeros_like(value)), axis), axis=0)
 
 
 def slot_lookup(keys, count):

time: 538 us -> 908 us (1.69)
  waiting for transfers between devices: 384 us -> 690 us
  other arithmetic: 12.9 us -> 73.5 us
    all_gather x0 -> x6, waiting for transfers between devices: none -> 690 us  [broadcast(): lax.all_gather(jnp.where(mine, value, jnp.zeros_like(value)), axis)]
    psum x4 -> x0, waiting for transfers between devices: 384 us -> none  [broadcast(): return lax.psum(jnp.where(mine, value, jnp.zeros_like(value)), axis)]
    reduce_sum x0 -> x6, other arithmetic: none -> 61.2 us  [broadcast(): jnp.sum(lax.all_gather(jnp.where(mine, value, jnp.zeros_like(value)), axi...]
  transfers between devices with their start and end apart: 4 -> 6, of which waited for: 4 -> 6; matrix products, arithmetic and copies ran while one was open for 10% -> 11% of each run, Pallas kernels for 0% -> 0%
where the time goes in v1:
time: 908 us; the launch traced here: 907 us
  waiting for transfers between devices  690 us (76%)
  local copies, waits for them, and re-layouts  96.8 us (11%)
  other arithmetic  73.5 us (8%)
  matrix products  32.7 us (4%)
  between operations  13.8 us (2%)
    all_gather x6, waiting for transfers between devices, broadcast(): lax.all_gather(jnp.where(mine, value, jnp.zeros_like(value)), axis)  690 us
    reduce_sum x6, other arithmetic, broadcast(): jnp.sum(lax.all_gather(jnp.where(mine, value, jnp.zeros_like(value)), axi...  61.2 us
    dot_general x2, matrix products, local(): jnp.einsum('sik,skj->sij', left, right, preferred_element_type=jnp.float32)  32 us
  transfers between devices with their start and end apart: 6, of which 6 were waited for; matrix products, arithmetic and copies ran while one was open for 11% of the time, Pallas kernels for 0%

profile of v1, /device:TPU:1, one launch (start us, length us, event | category | flops | bytes accessed | tf_op | source)
XLA Modules:
  0.0 906.8 jit_solution(6268613860860885243)
XLA Ops:
  16.0 4.3 gather_fusion.3
  27.7 85.7 %all-gather.9.cloned.1.call-done = bf16[16,128,4096]{2,1,0:T(8,128)(2,1)} async-done(((bf16[1,128,4096]{2,1,0:T(8,128)(2,1)}), bf16[16,128,4096]{2,1,0:T(8,128)(2,1)}) %all-gather.9.cloned.1.call-update) | async-done | bytes 16777232 | tf_op jit(solution)/shard_map/all_gather | solution.py:11
  113.3 8.9 reduce_sum.118
  122.3 86.9 %all-gather.11.cloned.1.call-done = bf16[16,128,4096]{2,1,0:T(8,128)(2,1)} async-done(((bf16[1,128,4096]{2,1,0:T(8,128)(2,1)}), bf16[16,128,4096]{2,1,0:T(8,128)(2,1)}) %all-gather.11.cloned.1.call-update) | async-done | bytes 16777232 | tf_op jit(solution)/shard_map/all_gather | solution.py:11
  209.2 9.9 %reduce_sum.119 = bf16[128,4096]{1,0:T(8,128)(2,1)} reduce(bf16[16,128,4096]{2,1,0:T(8,128)(2,1)} %all-gather.11.cloned.1.call-done, bf16[]{:T(256)} %constant.89.clone.1), dimensions={0}, to_apply=%region_4.5 | reduce | flops 7864320 | bytes 17825794 | tf_op jit(solution)/shard_map/reduce_sum | solution.py:11
  227.8 4.7 gather_fusion.2
  232.5 6.7 gather_fusion.6
  239.2 172.6 %all-gather.17.cloned.1.call-done = bf16[65536,256]{1,0:T(8,128)(2,1)} async-done(((bf16[4096,256]{1,0:T(8,128)(2,1)}), bf16[65536,256]{1,0:T(8,128)(2,1)}) %all-gather.17.cloned.1.call-update) | async-done | bytes 33554448 | tf_op jit(solution)/shard_map/all_gather | solution.py:11
  411.8 11.6 %reduce_sum.122 = bf16[4096,256]{1,0:T(8,128)(2,1)S(1)} reduce(bf16[16,4096,256]{2,1,0:T(8,128)(2,1)} %bitcast.160, bf16[]{:T(256)} %constant.89.clone.1), dimensions={0}, to_apply=%region_9.10 | reduce | flops 15728640 | bytes 35651584 | tf_op jit(solution)/shard_map/reduce_sum | solution.py:11
  429.0 4.7 gather_fusion.4
  433.7 6.6 gather_fusion.5
  440.3 16.1 %fusion.13 = bf16[128,128,128]{2,1,0:T(8,128)(2,1)} fusion(bf16[128,128,128]{2,1,0:T(8,128)(2,1)} %gather_fusion.2, bf16[128,128,128]{2,1,0:T(8,128)(2,1)} %gather_fusion.4, bf16[128,128,128]{2,1,0:T(8,128)(2,1)} %param.8, pred[128]{0:T(512)(128)(4,1)S(1)} %get-tuple-element.71, pred[128]{0:T(512)(128)(4,1)S(1)} %get-tuple-element.72, ...), kind=kOutput, calls=%fused_computation.31 | convolution fusion | flops 1086324736 | bytes 33554816 | tf_op jit(solution)/shard_map/sik,skj->sij/dot_general | solution.py:70
  464.1 4.4 gather_fusion.10
  471.9 85.4 %all-gather.13.cloned.1.call-done = bf16[16,128,4096]{2,1,0:T(8,128)(2,1)} async-done(((bf16[1,128,4096]{2,1,0:T(8,128)(2,1)}), bf16[16,128,4096]{2,1,0:T(8,128)(2,1)}) %all-gather.13.cloned.1.call-update) | async-done | bytes 16777232 | tf_op jit(solution)/shard_map/all_gather | solution.py:11
  557.3 9.2 %reduce_sum.125 = bf16[128,4096]{1,0:T(8,128)(2,1)S(1)} reduce(bf16[16,128,4096]{2,1,0:T(8,128)(2,1)} %all-gather.13.cloned.1.call-done, bf16[]{:T(256)} %constant.89.clone.1), dimensions={0}, to_apply=%region_11.12 | reduce | flops 7864320 | bytes 17825794 | tf_op jit(solution)/shard_map/reduce_sum | solution.py:11
  566.5 86.5 %all-gather.15.cloned.1.call-done = bf16[16,128,4096]{2,1,0:T(8,128)(2,1)} async-done(((bf16[1,128,4096]{2,1,0:T(8,128)(2,1)}), bf16[16,128,4096]{2,1,0:T(8,128)(2,1)}) %all-gather.15.cloned.1.call-update) | async-done | bytes 16777232 | tf_op jit(solution)/shard_map/all_gather | solution.py:11
  652.9 9.9 %reduce_sum.126 = bf16[128,4096]{1,0:T(8,128)(2,1)} reduce(bf16[16,128,4096]{2,1,0:T(8,128)(2,1)} %all-gather.15.cloned.1.call-done, bf16[]{:T(256)} %constant.89.clone.1), dimensions={0}, to_apply=%region_12.13 | reduce | flops 7864320 | bytes 17825794 | tf_op jit(solution)/shard_map/reduce_sum | solution.py:11
  671.6 6.6 gather_fusion.13
  678.2 4.7 gather_fusion.9
  682.9 172.5 %all-gather.19.cloned.1.call-done = bf16[65536,256]{1,0:T(8,128)(2,1)} async-done(((bf16[4096,256]{1,0:T(8,128)(2,1)}), bf16[65536,256]{1,0:T(8,128)(2,1)}) %all-gather.19.cloned.1.call-update) | async-done | bytes 33554448 | tf_op jit(solution)/shard_map/all_gather | solution.py:11
  855.5 11.6 %reduce_sum.129 = bf16[4096,256]{1,0:T(8,128)(2,1)S(1)} reduce(bf16[16,4096,256]{2,1,0:T(8,128)(2,1)} %bitcast.161, bf16[]{:T(256)} %constant.89.clone.1), dimensions={0}, to_apply=%region_17.18 | reduce | flops 15728640 | bytes 35651584 | tf_op jit(solution)/shard_map/reduce_sum | solution.py:11
  872.7 6.6 gather_fusion.12
  879.3 4.7 gather_fusion.11
  884.0 15.9 %fusion.11 = bf16[128,128,128]{2,1,0:T(8,128)(2,1)} fusion(bf16[128,128,128]{2,1,0:T(8,128)(2,1)} %gather_fusion.9, bf16[128,128,128]{2,1,0:T(8,128)(2,1)} %gather_fusion.11, bf16[128,128,128]{2,1,0:T(8,128)(2,1)} %fusion.13, pred[128]{0:T(512)(128)(4,1)S(1)} %get-tuple-element.70, pred[128]{0:T(512)(128)(4,1)S(1)} %get-tuple-element.68, ...), kind=kOutput, calls=%fused_computation.29 | convolution fusion | flops 1086324736 | bytes 33554816 | tf_op jit(solution)/shard_map/sik,skj->sij/dot_general | solution.py:70
  (77 shorter events, 59.4 us)
Async XLA Ops:
  6.5 106.8 %all-gather.9.cloned.1.call-start = ((), (), s32[]{:S(2)}) async-start(), calls=%async_computation | async-start | bytes 17825792 | tf_op jit(solution)/shard_map/all_gather | solution.py:11
  13.6 195.6 %all-gather.11.cloned.1.call-start = ((), (), s32[]{:S(2)}) async-start(), calls=%async_computation.1 | async-start | bytes 17825792 | tf_op jit(solution)/shard_map/all_gather | solution.py:11
  15.6 396.2 %all-gather.17.cloned.1.call-start = ((), (), s32[]{:S(2)}) async-start(), calls=%async_computation.4 | async-start | bytes 35651584 | tf_op jit(solution)/shard_map/all_gather | solution.py:11
  20.4 1.9 copy-start
  26.6 0.7 copy-start.2
  26.6 0.8 copy-start.1
  26.7 530.6 %all-gather.13.cloned.1.call-start = ((), (), s32[]{:S(2)}) async-start(), calls=%async_computation.2 | async-start | bytes 17825792 | tf_op jit(solution)/shard_map/all_gather | solution.py:11
  461.6 191.4 %all-gather.15.cloned.1.call-start = ((), (), s32[]{:S(2)}) async-start(), calls=%async_computation.3 | async-start | bytes 17825792 | tf_op jit(solution)/shard_map/all_gather | solution.py:11
  463.6 391.8 %all-gather.19.cloned.1.call-start = ((), (), s32[]{:S(2)}) async-start(), calls=%async_computation.5 | async-start | bytes 35651584 | tf_op jit(solution)/shard_map/all_gather | solution.py:11
Sparse Core Ops, SparseCore 0:
  13.7 99.6 all-gather.8
  115.2 93.9 all-gather.10
  211.6 200.1 all-gather.16
  461.7 95.5 all-gather.12
  559.0 93.9 all-gather.14
  655.2 200.1 all-gather.18
